TPU v7x, 256 devices: a whole 4x4x8 slice. The times are simulated.
256 devices in a mesh: freq: 8 (over z), bl: 32 (over y, x, core).
Axes of the slice: x: 4, y: 4, z: 8, core: 2. Of those that a mesh axis runs over, the one named last changes fastest.
Arguments:
- vis: float32 [2, 256, 65536], P(None, 'freq', 'bl'), may hold values from -60 to 60
- coherency: bfloat16 [2, 4, 256, 65536], P(None, None, 'freq', 'bl'), may hold values from -6 to 6
- gains_init: float32 [2, 4, 256, 512], P(None, None, 'freq', 'bl'), may hold values from -4 to 4
- station_pairs: int32 [2, 65536], P(None, 'bl'), may hold values from 0 to 511, as said below
Outputs:
- gains: float32 [2, 4, 256, 512], P(None, None, 'freq', 'bl')
- consensus: float32 [2, 4, 256, 512], P(None, None, 'freq', 'bl')
Inputs may be any that keep to these rules, and one draw needn't show every extreme that they name: `station_pairs`: in each column the two stations differ.
All inputs are finite; a program needn't handle non-finite values.
Results may differ from a plain program's by a relative error of at most 0.0013.
Values may be sent and summed in bfloat16 or wider, within the bound.
No kernel may reach another device: no remote copies, remote signals or barrier semaphores. Data moves between devices by JAX's collectives and lax.ppermute only.
A program may use at most 64 MiB of HBM per device.

v0:
```python
import jax
import jax.numpy as jnp
from jax import lax
from jax.sharding import PartitionSpec as P

STATION_TOTAL = 512
SKY_DIRECTIONS = 4
ITERS = 2
ROUNDS = 2


def basis_rows(channels):
    position = (2.0 * jnp.arange(channels, dtype=jnp.float32) + 1.0) / channels - 1.0
    raw = [jnp.ones_like(position), position, position * position, position * position * position]
    rows = []
    for vector in raw:
        for other in rows:
            vector = vector - jnp.sum(other * vector) * other
        rows.append(vector / jnp.sqrt(jnp.sum(vector * vector)))
    return jnp.stack(rows)


def model_terms(vis, coherency, near, far):
    coh_re = coherency[0].astype(jnp.float32)
    coh_im = coherency[1].astype(jnp.float32)
    z_re = coh_re * far[0] + coh_im * far[1]
    z_im = coh_im * far[0] - coh_re * far[1]
    x_re = near[0] * coh_re - near[1] * coh_im
    x_im = near[0] * coh_im + near[1] * coh_re
    model_re = jnp.sum(near[0] * z_re - near[1] * z_im, axis=0)
    model_im = jnp.sum(near[0] * z_im + near[1] * z_re, axis=0)
    res_re = (vis[0] - model_re)[None]
    res_im = (vis[1] - model_im)[None]
    first_terms = jnp.stack(
        [res_re * z_re + res_im * z_im, res_im * z_re - res_re * z_im, z_re * z_re + z_im * z_im]
    ).astype(jnp.bfloat16)
    second_terms = jnp.stack(
        [res_re * x_re + res_im * x_im, res_re * x_im - res_im * x_re, x_re * x_re + x_im * x_im]
    ).astype(jnp.bfloat16)
    return (first_terms, second_terms)


def advance(gains, sums, target, penalty_weight):
    return gains + (sums[0:2] + penalty_weight * (target - gains)) / (
        2.0 * sums[2] + penalty_weight
    )


def shards(vis, coherency, gains_init, station_pairs):
    channels_dev = vis.shape[1]
    rows_dev = vis.shape[2]
    owned = gains_init.shape[3]
    penalty_weight = 2.0 * rows_dev * lax.axis_size("bl") / STATION_TOTAL
    station_iota = jnp.arange(STATION_TOTAL, dtype=jnp.int32)
    first_table = (station_pairs[0][:, None] == station_iota[None, :]).astype(jnp.bfloat16)
    second_table = (station_pairs[1][:, None] == station_iota[None, :]).astype(jnp.bfloat16)
    whole_basis = basis_rows(channels_dev * lax.axis_size("freq"))
    local_basis = lax.dynamic_slice_in_dim(
        whole_basis, lax.axis_index("freq") * channels_dev, channels_dev, 1
    )
    width = 2 * SKY_DIRECTIONS * channels_dev
    term_width = 3 * SKY_DIRECTIONS * channels_dev
    contract_cols = (((1,), (1,)), ((), ()))
    contract_rows = (((0,), (1,)), ((), ()))
    gains = gains_init
    target = gains_init
    dual = jnp.zeros_like(gains_init)
    consensus = gains_init
    for round_index in range(ROUNDS):
        for step_index in range(ITERS):
            rounded = gains.astype(jnp.bfloat16).reshape(width, owned)
            piece = lax.all_gather(rounded, "bl", axis=1, tiled=True)
            near_part = lax.dot_general(
                piece, first_table, contract_cols, preferred_element_type=jnp.float32
            )
            far_part = lax.dot_general(
                piece, second_table, contract_cols, preferred_element_type=jnp.float32
            )
            first_terms, second_terms = model_terms(
                vis,
                coherency,
                near_part.reshape(2, SKY_DIRECTIONS, channels_dev, rows_dev),
                far_part.reshape(2, SKY_DIRECTIONS, channels_dev, rows_dev),
            )
            flat_first = first_terms.reshape(term_width, rows_dev)
            flat_second = second_terms.reshape(term_width, rows_dev)
            total = lax.dot_general(
                first_table, flat_first, contract_rows, preferred_element_type=jnp.float32
            )
            totals = lax.psum_scatter(
                total
                + lax.dot_general(
                    second_table, flat_second, contract_rows, preferred_element_type=jnp.float32
                ),
                "bl",
                scatter_dimension=0,
                tiled=True,
            )
            sums = totals.T.reshape(3, SKY_DIRECTIONS, channels_dev, owned)
            gains = advance(gains, sums, target, penalty_weight)
        blend = gains + dual
        partial_fit = jnp.einsum(
            "jk,adks->jads", local_basis, blend, precision=lax.Precision.HIGHEST
        )
        coefficients = lax.psum(partial_fit, "freq")
        consensus = jnp.einsum(
            "jk,jads->adks", local_basis, coefficients, precision=lax.Precision.HIGHEST
        )
        dual = dual + gains - consensus
        target = consensus - dual
    return (gains, consensus)


def solution(mesh):
    placed = (
        P(None, "freq", "bl"),
        P(None, None, "freq", "bl"),
        P(None, None, "freq", "bl"),
        P(None, "bl"),
    )
    return jax.shard_map(
        shards,
        mesh=mesh,
        in_specs=placed,
        out_specs=(P(None, None, "freq", "bl"), P(None, None, "freq", "bl")),
        check_vma=False,
    )
```

profile of v0, /device:TPU:2, one launch (start us, length us, event | category | flops | bytes accessed | tf_op | source)
XLA Modules:
  0.0 535.2 jit_solution(11720419480373013828)
XLA Ops:
  9.0 24.8 %all_gather.12 = bf16[256,512]{0,1:T(8,128)(2,1)S(1)} all-gather(bf16[256,16]{0,1:T(8,128)(2,1)S(1)} %reshape.258), channel_id=1, replica_groups=mesh['freq'=8,'bl'=32] {'bl'}, dimensions={1}, use_global_device_ids=true | all-gather | bytes 270336 | tf_op jit(solution)/shard_map/all_gather | solution.py:72
  33.8 1.4 fusion.43
  36.7 1.4 fusion.42
  41.6 1.7 fusion.11
  43.3 2.6 fusion.60
  46.0 85.9 %reduce-scatter.5.cloned.1.call-done = f32[16,384]{1,0:T(8,128)} async-done(((f32[512,384]{1,0:T(8,128)}), f32[16,384]{1,0:T(8,128)}) %reduce-scatter.5.cloned.1.call-update) | async-done | bytes 24592 | tf_op jit(solution)/shard_map/reduce_scatter | solution.py:90
  133.7 23.6 %all_gather.13 = bf16[256,512]{0,1:T(8,128)(2,1)S(1)} all-gather(bf16[256,16]{0,1:T(8,128)(2,1)S(1)} %reshape.259), channel_id=1, replica_groups=mesh['freq'=8,'bl'=32] {'bl'}, dimensions={1}, use_global_device_ids=true | all-gather | bytes 270336 | tf_op jit(solution)/shard_map/all_gather | solution.py:72
  163.6 1.7 fusion.9
  165.5 2.6 fusion.63
  168.2 84.8 %reduce-scatter.7.cloned.1.call-done = f32[16,384]{1,0:T(8,128)} async-done(((f32[512,384]{1,0:T(8,128)}), f32[16,384]{1,0:T(8,128)}) %reduce-scatter.7.cloned.1.call-update) | async-done | bytes 24592 | tf_op jit(solution)/shard_map/reduce_scatter | solution.py:90
  254.8 23.3 %all_gather.14 = bf16[256,512]{0,1:T(8,128)(2,1)S(1)} all-gather(bf16[256,16]{0,1:T(8,128)(2,1)S(1)} %reshape.260), channel_id=1, replica_groups=mesh['freq'=8,'bl'=32] {'bl'}, dimensions={1}, use_global_device_ids=true | all-gather | bytes 270336 | tf_op jit(solution)/shard_map/all_gather | solution.py:72
  280.0 1.4 fusion.13
  284.4 1.7 fusion.7
  286.3 2.6 fusion.66
  296.7 1.9 multiply_reduce_fusion.1
  298.6 2.6 multiply_reduce_fusion
  301.9 2.0 fusion.128
  304.5 30.2 %psum.14 = f32[4,2,4,16]{3,0,2,1:T(4,128)S(1)} all-reduce(f32[4,2,4,16]{3,0,2,1:T(4,128)S(1)} %fusion.159), channel_id=1, replica_groups=mesh['freq'=8,'bl'=32] {'freq'}, use_global_device_ids=true, to_apply=%region_18.0 | all-reduce | flops 512 | bytes 4096 | tf_op jit(solution)/shard_map/psum | solution.py:105
  334.7 39.2 %reduce-scatter.9.cloned.1.call-done = f32[16,384]{1,0:T(8,128)} async-done(((f32[512,384]{1,0:T(8,128)}), f32[16,384]{1,0:T(8,128)}) %reduce-scatter.9.cloned.1.call-update) | async-done | bytes 24592 | tf_op jit(solution)/shard_map/reduce_scatter | solution.py:90
  375.9 23.3 %all_gather.15 = bf16[256,512]{0,1:T(8,128)(2,1)S(1)} all-gather(bf16[256,16]{0,1:T(8,128)(2,1)S(1)} %reshape.261), channel_id=1, replica_groups=mesh['freq'=8,'bl'=32] {'bl'}, dimensions={1}, use_global_device_ids=true | all-gather | bytes 270336 | tf_op jit(solution)/shard_map/all_gather | solution.py:72
  405.5 1.7 fusion.5
  407.4 2.6 fusion.69
  410.1 84.9 %reduce-scatter.11.cloned.1.call-done = f32[16,384]{1,0:T(8,128)} async-done(((f32[512,384]{1,0:T(8,128)}), f32[16,384]{1,0:T(8,128)}) %reduce-scatter.11.cloned.1.call-update) | async-done | bytes 24592 | tf_op jit(solution)/shard_map/reduce_scatter | solution.py:90
  497.2 30.3 %psum.15 = f32[4,2,4,16]{3,0,2,1:T(4,128)S(1)} all-reduce(f32[4,2,4,16]{3,0,2,1:T(4,128)S(1)} %fusion.112), channel_id=1, replica_groups=mesh['freq'=8,'bl'=32] {'freq'}, use_global_device_ids=true, to_apply=%region_22.0 | all-reduce | flops 512 | bytes 4096 | tf_op jit(solution)/shard_map/psum | solution.py:105
  (102 shorter events, 38.3 us)
Async XLA Ops:
  7.2 124.8 %reduce-scatter.5.cloned.1.call-start = ((), (), s32[]{:S(2)}) async-start(), calls=%async_computation.4 | async-start | bytes 811008 | tf_op jit(solution)/shard_map/reduce_scatter | solution.py:90
  35.2 1.2 copy-start
  38.3 1.0 copy-start.1
  43.3 90.2 %copy-start.2 = (f32[2,4,32,16]{2,3,1,0:T(8,128)S(1)}, f32[2,4,32,16]{2,3,1,0:T(8,128)}, u32[]{:S(2)}) copy-start(f32[2,4,32,16]{2,3,1,0:T(8,128)} %param.6) | copy-start | bytes 49156
  46.0 207.0 %reduce-scatter.7.cloned.1.call-start = ((), (), s32[]{:S(2)}) async-start(), calls=%async_computation.5 | async-start | bytes 811008 | tf_op jit(solution)/shard_map/reduce_scatter | solution.py:90
  168.1 205.7 %reduce-scatter.9.cloned.1.call-start = ((), (), s32[]{:S(2)}) async-start(), calls=%async_computation.6 | async-start | bytes 811008 | tf_op jit(solution)/shard_map/reduce_scatter | solution.py:90
  288.9 206.1 %reduce-scatter.11.cloned.1.call-start = ((), (), s32[]{:S(2)}) async-start(), calls=%async_computation.7 | async-start | bytes 811008 | tf_op jit(solution)/shard_map/reduce_scatter | solution.py:90
  496.6 31.8 %copy-start.3 = (f32[2,4,32,16]{2,3,1,0:T(8,128)}, f32[2,4,32,16]{2,3,1,0:T(8,128)S(1)}, u32[]{:S(2)}) copy-start(f32[2,4,32,16]{2,3,1,0:T(8,128)S(1)} %fusion.105) | copy-start | bytes 49156
Sparse Core Ops, SparseCore 0:
  46.1 85.8 reduce-scatter.4
  168.2 84.7 reduce-scatter.6
  289.0 84.7 reduce-scatter.8
  410.2 84.7 reduce-scatter.10
where the time goes:
time: 543 us; the launch traced here: 535 us
  waiting for transfers between devices  295 us (54%)
  blocking collectives  155 us (29%)
  matrix products  31 us (6%)
  other arithmetic  27.4 us (5%)
  between operations  18.5 us (3%)
  local copies, waits for them, and re-layouts  7.82 us (1%)
    reduce_scatter x4, waiting for transfers between devices, shards(): lax.psum_scatter(total + lax.dot_general(second_table, flat_second, contr...  295 us
    all_gather x4, blocking collectives, shards(): piece = lax.all_gather(rounded, 'bl', axis=1, tiled=True)  95 us
    psum x2, blocking collectives, shards(): coefficients = lax.psum(partial_fit, 'freq')  60.5 us
  transfers between devices with their start and end apart: 4, of which 4 were waited for; matrix products, arithmetic and copies ran while one was open for 2% of the time, Pallas kernels for 0%

commit v1 on v0

--- a/solution.py
+++ b/solution.py
@@ -69,7 +69,9 @@
     for round_index in range(ROUNDS):
         for step_index in range(ITERS):
             rounded = gains.astype(jnp.bfloat16).reshape(width, owned)
-            piece = lax.all_gather(rounded, "bl", axis=1, tiled=True)
+            piece = jnp.concatenate(
+                lax.all_to_all(jnp.stack([rounded] * lax.axis_size("bl")), "bl", 0, 0), axis=1
+            )
             near_part = lax.dot_general(
                 piece, first_table, contract_cols, preferred_element_type=jnp.float32
             )

time: 543 us -> 492 us (0.906); the launches traced: 535 us -> 491 us
  blocking collectives: 155 us -> 100 us
  starting transfers between devices: 0.16 us -> 7.79 us
    all_gather x4 -> x0, blocking collectives: 95 us -> none  [shards(): piece = lax.all_gather(rounded, 'bl', axis=1, tiled=True)]
    all_to_all x0 -> x3, blocking collectives: none -> 39.9 us  [shards(): lax.all_to_all(jnp.stack([rounded] * lax.axis_size('bl')), 'bl', 0, 0)]
    all_to_all x0 -> x1, starting transfers between devices: none -> 7.62 us  [shards(): lax.all_to_all(jnp.stack([rounded] * lax.axis_size('bl')), 'bl', 0, 0)]
    all_to_all x0 -> x1, waiting for transfers between devices: none -> 6.82 us  [shards(): lax.all_to_all(jnp.stack([rounded] * lax.axis_size('bl')), 'bl', 0, 0)]
  transfers between devices with their start and end apart: 4 -> 5, of which waited for: 4 -> 5; matrix products, arithmetic and copies ran while one was open for 2% -> 3% of each run, Pallas kernels for 0% -> 0%
where the time goes in v1:
time: 492 us; the launch traced here: 491 us
  waiting for transfers between devices  297 us (60%)
  blocking collectives  100 us (20%)
  matrix products  31 us (6%)
  other arithmetic  27.4 us (6%)
  between operations  18.3 us (4%)
  local copies, waits for them, and re-layouts  8.6 us (2%)
  starting transfers between devices  7.79 us (2%)
    reduce_scatter x4, waiting for transfers between devices, shards(): lax.psum_scatter(total + lax.dot_general(second_table, flat_second, contr...  291 us
    psum x2, blocking collectives, shards(): coefficients = lax.psum(partial_fit, 'freq')  60.4 us
    all_to_all x3, blocking collectives, shards(): lax.all_to_all(jnp.stack([rounded] * lax.axis_size('bl')), 'bl', 0, 0)  39.9 us
    dot_general x4, matrix products, shards(): lax.dot_general(first_table, flat_first, contract_rows, preferred_element...  10.4 us
  transfers between devices with their start and end apart: 5, of which 5 were waited for; matrix products, arithmetic and copies ran while one was open for 3% of the time, Pallas kernels for 0%

profile of v1, /device:TPU:2, one launch (start us, length us, event | category | flops | bytes accessed | tf_op | source)
XLA Modules:
  0.0 490.8 jit_solution(1690603841217418606)
XLA Ops:
  8.8 7.6 %all-to-all-start = ((bf16[32,256,16]{1,2,0:T(8,128)(2,1)}), bf16[32,256,16]{1,2,0:T(8,128)(2,1)S(1)}, u32[]{:S(2)}, u32[]{:S(2)}) async-start(bf16[32,256,16]{1,2,0:T(8,128)(2,1)} %stack.36), calls=%async_computation | async-start | bytes 524288 | tf_op jit(solution)/shard_map/all_to_all | solution.py:73
  17.3 6.8 %all-to-all-done = bf16[32,256,16]{1,2,0:T(8,128)(2,1)S(1)} async-done(((bf16[32,256,16]{1,2,0:T(8,128)(2,1)}), bf16[32,256,16]{1,2,0:T(8,128)(2,1)S(1)}, u32[]{:S(2)}, u32[]{:S(2)}) %all-to-all-start) | async-done | bytes 262176 | tf_op jit(solution)/shard_map/all_to_all | solution.py:73
  24.1 1.4 fusion.43
  27.1 1.4 fusion.42
  32.0 1.7 fusion.11
  33.7 2.6 fusion.60
  36.4 85.1 %reduce-scatter.5.cloned.1.call-done = f32[16,384]{1,0:T(8,128)} async-done(((f32[512,384]{1,0:T(8,128)}), f32[16,384]{1,0:T(8,128)}) %reduce-scatter.5.cloned.1.call-update) | async-done | bytes 24592 | tf_op jit(solution)/shard_map/reduce_scatter | solution.py:92
  123.3 13.3 %all_to_all.20 = bf16[32,256,16]{1,2,0:T(8,128)(2,1)S(1)} all-to-all(bf16[32,256,16]{1,2,0:T(8,128)(2,1)S(1)} %stack.39), channel_id=1, replica_groups=mesh['freq'=8,'bl'=32] {'bl'}, dimensions={0} | all-to-all | bytes 524288 | tf_op jit(solution)/shard_map/all_to_all | solution.py:73
  142.9 1.7 fusion.9
  144.9 2.6 fusion.63
  147.5 83.7 %reduce-scatter.7.cloned.1.call-done = f32[16,384]{1,0:T(8,128)} async-done(((f32[512,384]{1,0:T(8,128)}), f32[16,384]{1,0:T(8,128)}) %reduce-scatter.7.cloned.1.call-update) | async-done | bytes 24592 | tf_op jit(solution)/shard_map/reduce_scatter | solution.py:92
  233.0 13.3 %all_to_all.21 = bf16[32,256,16]{1,2,0:T(8,128)(2,1)S(1)} all-to-all(bf16[32,256,16]{1,2,0:T(8,128)(2,1)S(1)} %stack.83), channel_id=1, replica_groups=mesh['freq'=8,'bl'=32] {'bl'}, dimensions={0} | all-to-all | bytes 524288 | tf_op jit(solution)/shard_map/all_to_all | solution.py:73
  252.6 1.7 fusion.7
  254.5 2.6 fusion.66
  264.9 1.9 multiply_reduce_fusion.1
  266.8 2.6 multiply_reduce_fusion
  270.1 2.0 fusion.128
  272.7 30.2 %psum.14 = f32[4,2,4,16]{3,0,2,1:T(4,128)S(1)} all-reduce(f32[4,2,4,16]{3,0,2,1:T(4,128)S(1)} %fusion.159), channel_id=1, replica_groups=mesh['freq'=8,'bl'=32] {'freq'}, use_global_device_ids=true, to_apply=%region_18.0 | all-reduce | flops 512 | bytes 4096 | tf_op jit(solution)/shard_map/psum | solution.py:107
  302.9 38.0 %reduce-scatter.9.cloned.1.call-done = f32[16,384]{1,0:T(8,128)} async-done(((f32[512,384]{1,0:T(8,128)}), f32[16,384]{1,0:T(8,128)}) %reduce-scatter.9.cloned.1.call-update) | async-done | bytes 24592 | tf_op jit(solution)/shard_map/reduce_scatter | solution.py:92
  343.0 13.3 %all_to_all.22 = bf16[32,256,16]{1,2,0:T(8,128)(2,1)S(1)} all-to-all(bf16[32,256,16]{1,2,0:T(8,128)(2,1)S(1)} %stack.88), channel_id=1, replica_groups=mesh['freq'=8,'bl'=32] {'bl'}, dimensions={0} | all-to-all | bytes 524288 | tf_op jit(solution)/shard_map/all_to_all | solution.py:73
  362.6 1.7 fusion.5
  364.5 2.6 fusion.69
  367.1 83.8 %reduce-scatter.11.cloned.1.call-done = f32[16,384]{1,0:T(8,128)} async-done(((f32[512,384]{1,0:T(8,128)}), f32[16,384]{1,0:T(8,128)}) %reduce-scatter.11.cloned.1.call-update) | async-done | bytes 24592 | tf_op jit(solution)/shard_map/reduce_scatter | solution.py:92
  453.1 30.2 %psum.15 = f32[4,2,4,16]{3,0,2,1:T(4,128)S(1)} all-reduce(f32[4,2,4,16]{3,0,2,1:T(4,128)S(1)} %fusion.112), channel_id=1, replica_groups=mesh['freq'=8,'bl'=32] {'freq'}, use_global_device_ids=true, to_apply=%region_22.0 | all-reduce | flops 512 | bytes 4096 | tf_op jit(solution)/shard_map/psum | solution.py:107
  (107 shorter events, 40.5 us)
Async XLA Ops:
  8.8 15.3 %all-to-all-start = ((bf16[32,256,16]{1,2,0:T(8,128)(2,1)}), bf16[32,256,16]{1,2,0:T(8,128)(2,1)S(1)}, u32[]{:S(2)}, u32[]{:S(2)}) async-start(bf16[32,256,16]{1,2,0:T(8,128)(2,1)} %stack.36), calls=%async_computation | async-start | bytes 524288 | tf_op jit(solution)/shard_map/all_to_all | solution.py:73
  16.5 105.1 %reduce-scatter.5.cloned.1.call-start = ((), (), s32[]{:S(2)}) async-start(), calls=%async_computation.8 | async-start | bytes 811008 | tf_op jit(solution)/shard_map/reduce_scatter | solution.py:92
  25.6 1.2 copy-start
  28.7 1.0 copy-start.1
  33.7 89.4 %copy-start.2 = (f32[2,4,32,16]{2,3,1,0:T(8,128)S(1)}, f32[2,4,32,16]{2,3,1,0:T(8,128)}, u32[]{:S(2)}) copy-start(f32[2,4,32,16]{2,3,1,0:T(8,128)} %param.6) | copy-start | bytes 49156
  36.3 194.9 %reduce-scatter.7.cloned.1.call-start = ((), (), s32[]{:S(2)}) async-start(), calls=%async_computation.9 | async-start | bytes 811008 | tf_op jit(solution)/shard_map/reduce_scatter | solution.py:92
  147.5 193.4 %reduce-scatter.9.cloned.1.call-start = ((), (), s32[]{:S(2)}) async-start(), calls=%async_computation.10 | async-start | bytes 811008 | tf_op jit(solution)/shard_map/reduce_scatter | solution.py:92
  257.1 193.7 %reduce-scatter.11.cloned.1.call-start = ((), (), s32[]{:S(2)}) async-start(), calls=%async_computation.11 | async-start | bytes 811008 | tf_op jit(solution)/shard_map/reduce_scatter | solution.py:92
  452.5 31.7 %copy-start.3 = (f32[2,4,32,16]{2,3,1,0:T(8,128)}, f32[2,4,32,16]{2,3,1,0:T(8,128)S(1)}, u32[]{:S(2)}) copy-start(f32[2,4,32,16]{2,3,1,0:T(8,128)S(1)} %fusion.105) | copy-start | bytes 49156
Sparse Core Ops, SparseCore 0:
  36.5 85.0 reduce-scatter.4
  147.6 83.5 reduce-scatter.6
  257.3 83.5 reduce-scatter.8
  367.2 83.5 reduce-scatter.10
